TPU v7x, 32 devices: a whole 2x2x4 slice. The times are simulated.
32 devices in a mesh: span: 4 (over y, x), tensor: 8 (over z, core).
Axes of the slice: x: 2, y: 2, z: 4, core: 2. Of those that a mesh axis runs over, the one named last changes fastest.
Arguments:
- tokens: bfloat16 [1024, 4096], P('span', 'tensor'), may hold values from -200 to 200
- retain: float32 [1024], P('span'), may hold values from 0.5 to 1
- norm_gain: float32 [4096], P('tensor'), may hold values from 0.1 to 1.9
- norm_bias: float32 [4096], P('tensor'), may hold values from -2.5 to 2.5
- decay_rate: float32 [16, 4096], P(None, 'tensor'), may hold values from 0.00024414062 to 0.0333333333
- ema_angle: float32 [16, 4096], P(None, 'tensor'), may hold values from -0.05 to 0.05
- ema_input: float32 [16, 4096], P(None, 'tensor'), may hold values from -2.4 to 2.4
- ema_output: float32 [2, 16, 4096], P(None, None, 'tensor'), may hold values from -0.25 to 0.25
- ema_skip: float32 [4096], P('tensor'), may hold values from -3 to 3
- shared_weight: bfloat16 [4096, 1024], P('tensor'), may hold values from -0.125 to 0.125
- shared_gain: float32 [1024], replicated, may hold values from 0.1 to 1.9
- output_weight: bfloat16 [1024, 4096], P(None, 'tensor'), may hold values from -0.1875 to 0.1875
Outputs:
- layer_out: bfloat16 [1024, 4096], P('span', 'tensor')
All inputs are finite; a program needn't handle non-finite values.
Results may differ from a plain program's by a relative error of at most 0.02.
Values may be sent and summed in bfloat16 or wider, within the bound.
A program may use at most 128 MiB of HBM per device.

v0:
```python
import functools

import jax
import jax.numpy as jnp
from jax import lax
from jax.experimental import pallas as pl
from jax.experimental.pallas import tpu as pltpu
from jax.sharding import PartitionSpec as P

GROUP = 64
STEPS = 8
LANES = 128
NORM_EPS = 1e-05
SCALE_EPS = 1e-06

MESH = pl.DeviceIdType.MESH
VMEM = pl.BlockSpec(memory_space=pltpu.VMEM)


def dot(a, b):
    return jnp.dot(a, b, preferred_element_type=jnp.float32)


def pieces(values, count):
    out = []
    for _ in range(count):
        piece = values.astype(jnp.bfloat16)
        out.append(piece)
        values = values - piece.astype(jnp.float32)
    return out


def group_ones(channels):
    row = lax.broadcasted_iota(jnp.int32, (channels, channels), 0) // GROUP
    column = lax.broadcasted_iota(jnp.int32, (channels, channels), 1) // GROUP
    return (row == column).astype(jnp.bfloat16)


def remote(source, target, send_sem, recv_sem, axis, device):
    return pltpu.make_async_remote_copy(
        src_ref=source,
        dst_ref=target,
        send_sem=send_sem,
        recv_sem=recv_sem,
        device_id={axis: device},
        device_id_type=MESH,
    )


def to_later(count, pairs, send_sem, recv_sem):
    me = lax.axis_index("span")
    for step in range(1, count):

        @pl.when(me + step < count)
        def _():
            for item, (source, landing) in enumerate(pairs):
                remote(source, landing.at[me], send_sem.at[item, step - 1], recv_sem.at[item, step - 1], "span", me + step).start()


def from_earlier(count, pairs, send_sem, recv_sem):
    me = lax.axis_index("span")
    for step in range(1, count):

        @pl.when(me >= step)
        def _():
            for item, (source, landing) in enumerate(pairs):
                remote(source, landing.at[me], send_sem.at[item, step - 1], recv_sem.at[item, step - 1], "span", me - step).wait_recv()

        @pl.when(me + step < count)
        def _():
            for item, (source, landing) in enumerate(pairs):
                remote(source, landing.at[me], send_sem.at[item, step - 1], recv_sem.at[item, step - 1], "span", me + step).wait_send()


def wide(column, width):
    return jnp.concatenate([column] * (width // LANES), axis=1)


def lanes_of(channels, width):
    return [slice(start, start + width) for start in range(0, channels, width)]


def layer_kernel(
    count,
    chips,
    tokens_ref,
    retain_ref,
    norm_gain_ref,
    bias_ref,
    rate_ref,
    angle_ref,
    input_ref,
    output_ref,
    skip_ref,
    gain_ref,
    weight_hbm,
    mixer_hbm,
    out_ref,
    weight_ref,
    mixer_ref,
    total_ref,
    totals_ref,
    before_ref,
    normed_ref,
    scaled_ref,
    prefix_ref,
    power_ref,
    unit_ref,
    read_ref,
    start_ref,
    state_ref,
    states_ref,
    kept_ref,
    kepts_ref,
    ema_ref,
    part_ref,
    near_ref,
    sum_ref,
    far_ref,
    own_ref,
    all_ref,
    load_sem,
    total_send,
    total_recv,
    state_send,
    state_recv,
    pair_send,
    pair_recv,
    far_send,
    far_recv,
    out_send,
    out_recv,
    back_send,
    back_recv,
):
    length, channels = tokens_ref.shape
    ndim = rate_ref.shape[0]
    blocks = length // STEPS
    halves, rows = part_ref.shape[2:4]
    span = lax.axis_index("span")
    me = lax.axis_index("tensor")
    core = lax.rem(me, 2)
    chip = lax.div(me, 2)
    partner = me + 1 - 2 * core
    order = [lax.rem(chip + step, chips) for step in range(1, chips)] + [chip]
    peers = [2 * place + core for place in order[:-1]]

    barrier = pltpu.get_barrier_semaphore()
    for step in range(1, count):
        pl.semaphore_signal(barrier, inc=1, device_id={"span": lax.rem(span + step, count)}, device_id_type=MESH)
    for peer in [partner] + peers:
        pl.semaphore_signal(barrier, inc=1, device_id={"tensor": peer}, device_id_type=MESH)
    loads = [
        pltpu.make_async_copy(weight_hbm, weight_ref, load_sem.at[0]),
        pltpu.make_async_copy(mixer_hbm, mixer_ref, load_sem.at[1]),
    ]
    for load in loads:
        load.start()

    tokens = tokens_ref[...]
    values = tokens.astype(jnp.float32)
    ones = group_ones(channels)
    total = jnp.sum(values, axis=0, keepdims=True)
    squares = jnp.sum(values * values, axis=0, keepdims=True)
    summed = jnp.concatenate([total, squares, jnp.zeros((6, channels), jnp.float32)], axis=0)
    total_ref[...] = sum(dot(piece, ones) for piece in pieces(summed, 3))
    pl.semaphore_wait(barrier, count - 1 + chips)
    stats_pairs = [(total_ref, totals_ref)]
    to_later(count, stats_pairs, total_send, total_recv)

    rate, angle = rate_ref[...], angle_ref[...]
    size = jnp.exp(-rate)
    turn_re = size * jnp.cos(angle)
    turn_im = size * jnp.sin(angle)
    weight = (1.0 - size) * input_ref[...]
    read_re = weight * output_ref[0]
    read_im = weight * output_ref[1]
    power_re, power_im = jnp.ones_like(rate), jnp.zeros_like(rate)
    lag_rows = []
    for lag in range(STEPS + 1):
        if lag < STEPS:
            lag_rows.append(jnp.sum(read_re * power_re - read_im * power_im, axis=0, keepdims=True))
        power_ref[0, lag] = power_re
        power_ref[1, lag] = power_im
        power_re, power_im = power_re * turn_re - power_im * turn_im, power_re * turn_im + power_im * turn_re
    unit_ref[0] = read_re * turn_re - read_im * turn_im
    unit_ref[1] = read_re * turn_im + read_im * turn_re
    step_row = lax.broadcasted_iota(jnp.int32, (STEPS, channels), 0)

    def table(part, carried):
        here = pl.ds(part, 1)
        re = jnp.broadcast_to(unit_ref[0, here, :], (STEPS, channels))
        im = jnp.broadcast_to(unit_ref[1, here, :], (STEPS, channels))
        for bit in (1, 2, 4):
            chosen = (step_row // bit) % 2 == 1
            by_re = jnp.where(chosen, jnp.broadcast_to(power_ref[0, bit, here, :], (STEPS, channels)), 1.0)
            by_im = jnp.where(chosen, jnp.broadcast_to(power_ref[1, bit, here, :], (STEPS, channels)), 0.0)
            re, im = re * by_re - im * by_im, re * by_im + im * by_re
        read_ref[0, part] = re
        read_ref[1, part] = im
        return carried

    lax.fori_loop(0, ndim, table, 0)

    sums = dot(tokens, ones)
    squares = sum(dot(piece, ones) for piece in pieces(values * values, 2))
    row = lax.broadcasted_iota(jnp.int32, (length, length), 0)
    column = lax.broadcasted_iota(jnp.int32, (length, length), 1)
    lower = (column <= row).astype(jnp.bfloat16)
    cum_sum = sum(dot(lower, piece) for piece in pieces(sums, 3))
    cum_sq = sum(dot(lower, piece) for piece in pieces(squares, 3))
    diagonal = jnp.where(row == column, jnp.broadcast_to(retain_ref[...], (length, length)), 0.0)
    keep = sum(dot(piece, jnp.ones((length, LANES), jnp.bfloat16)) for piece in pieces(diagonal, 3))
    place_in = lax.broadcasted_iota(jnp.int32, (length, LANES), 0) % STEPS
    prefix = keep
    suffix = jnp.where(place_in < STEPS - 1, pltpu.roll(keep, length - 1, 0), 1.0)
    for by in (1, 2, 4):
        prefix = jnp.where(place_in >= by, prefix * pltpu.roll(prefix, by, 0), prefix)
        suffix = jnp.where(place_in + by < STEPS, suffix * pltpu.roll(suffix, length - by, 0), suffix)
    prefix_ref[...] = prefix
    position = lax.broadcasted_iota(jnp.int32, (length, channels), 0)
    counts = ((span * length + position + 1) * GROUP).astype(jnp.float32)

    from_earlier(count, stats_pairs, total_send, total_recv)
    before_ref[...] = jnp.zeros((8, channels), jnp.float32)
    for other in range(count - 1):

        @pl.when(other < span)
        def _():
            before_ref[...] += totals_ref[other]

    average = (before_ref[0:1] + cum_sum) / counts
    spread = (before_ref[1:2] + cum_sq) / counts - average * average
    inverse = lax.rsqrt(spread + NORM_EPS)
    normed = (values - average) * inverse * norm_gain_ref[...] + bias_ref[...]
    normed_ref[...] = normed
    scaled_ref[...] = normed * wide(suffix, channels)

    width = min(512, channels)
    for lanes in lanes_of(channels, width):
        whole_re, whole_im = power_ref[0, STEPS, :, lanes], power_ref[1, STEPS, :, lanes]

        def enter(block, carried):
            re, im, kept = carried
            start_ref[0, block, :, lanes] = re
            start_ref[1, block, :, lanes] = im
            first = pl.multiple_of(block * STEPS, STEPS)
            factor = wide(prefix_ref[pl.ds(first + STEPS - 1, 1), :], width)
            add_re = jnp.broadcast_to(scaled_ref[pl.ds(first + STEPS - 1, 1), lanes], (ndim, width))
            add_im = jnp.zeros((ndim, width), jnp.float32)
            for step in range(STEPS - 1):
                entry = scaled_ref[pl.ds(first + step, 1), lanes]
                lag = STEPS - 1 - step
                add_re = add_re + power_ref[0, lag, :, lanes] * entry
                add_im = add_im + power_ref[1, lag, :, lanes] * entry
            next_re = (whole_re * re - whole_im * im) * factor + add_re
            next_im = (whole_re * im + whole_im * re) * factor + add_im
            return next_re, next_im, kept * factor

        zero = jnp.zeros((ndim, width), jnp.float32)
        re, im, kept = lax.fori_loop(0, blocks, enter, (zero, zero, jnp.ones((1, width), jnp.float32)))
        state_ref[0:ndim, lanes] = re.astype(state_ref.dtype)
        state_ref[ndim : 2 * ndim, lanes] = im.astype(state_ref.dtype)
    kept_ref[...] = jnp.broadcast_to(kept[:, :LANES], (8, LANES))
    state_pairs = [(state_ref, states_ref), (kept_ref, kepts_ref)]
    to_later(count, state_pairs, state_send, state_recv)

    for lanes in lanes_of(channels, LANES):
        reach = jnp.where(place_in >= 0, 1.0, 0.0)
        here = normed_ref[:, lanes]
        within = here * lag_rows[0][:, lanes]
        for lag in range(1, STEPS):
            reach = jnp.where(place_in >= lag, reach * (pltpu.roll(keep, lag - 1, 0) if lag > 1 else keep), 0.0)
            within = within + pltpu.roll(here, lag, 0) * (lag_rows[lag][:, lanes] * reach)
        ema_ref[:, lanes] = within + skip_ref[:, lanes] * here

    from_earlier(count, state_pairs, state_send, state_recv)
    whole = jnp.exp(-rate * length)
    unit_ref[0] = whole * jnp.cos(angle * length)
    unit_ref[1] = whole * jnp.sin(angle * length)
    power_ref[0, 0] = jnp.zeros_like(rate)
    power_ref[1, 0] = jnp.zeros_like(rate)
    for other in range(count - 1):

        @pl.when(other < span)
        def _():
            kept = wide(kepts_ref[other, 0:1, :], channels)
            re, im = power_ref[0, 0], power_ref[1, 0]
            by_re, by_im = unit_ref[0], unit_ref[1]
            power_ref[0, 0] = (by_re * re - by_im * im) * kept + states_ref[other, 0:ndim].astype(jnp.float32)
            power_ref[1, 0] = (by_re * im + by_im * re) * kept + states_ref[other, ndim : 2 * ndim].astype(jnp.float32)

    width = min(256, channels)
    for lanes in lanes_of(channels, width):
        whole_re, whole_im = power_ref[0, STEPS, :, lanes], power_ref[1, STEPS, :, lanes]

        def leave(block, carried):
            re, im = carried
            first = pl.multiple_of(block * STEPS, STEPS)
            parts = [jnp.zeros((STEPS, width), jnp.float32) for _ in range(4)]
            for part in range(ndim):
                here = pl.ds(part, 1)
                slot = 2 * (part % 2)
                parts[slot] = parts[slot] + read_ref[0, part, :, lanes] * start_ref[0, block, here, lanes]
                parts[slot + 1] = parts[slot + 1] + read_ref[1, part, :, lanes] * start_ref[1, block, here, lanes]
            read = (parts[0] - parts[1]) + (parts[2] - parts[3])
            ema_ref[pl.ds(first, STEPS), lanes] += read * wide(prefix_ref[pl.ds(first, STEPS), :], width)
            factor = wide(prefix_ref[pl.ds(first + STEPS - 1, 1), :], width)
            re, im = (whole_re * re - whole_im * im) * factor, (whole_re * im + whole_im * re) * factor
            start_ref[0, block + 1, :, lanes] += re
            start_ref[1, block + 1, :, lanes] += im
            return re, im

        re, im = power_ref[0, 0, :, lanes], power_ref[1, 0, :, lanes]
        start_ref[0, 0, :, lanes] += re
        start_ref[1, 0, :, lanes] += im
        start_ref[0, blocks, :, lanes] = re
        start_ref[1, blocks, :, lanes] = im
        lax.fori_loop(0, blocks, leave, (re, im), unroll=2)

    ema = ema_ref[...]
    active = (ema / (1.0 + jnp.exp(-ema))).astype(jnp.bfloat16)
    for load in loads:
        load.wait()
    product = dot(active, weight_ref[...]).astype(jnp.bfloat16)
    part_ref[...] = product.reshape(part_ref.shape)

    pair, far, outward, home, back = {}, {}, {}, {}, {}
    for half in range(halves):
        for slot, place in enumerate(order):
            copy = remote(part_ref.at[place, 1 - core, half], near_ref.at[slot, half], pair_send.at[slot, half], pair_recv.at[slot, half], "tensor", partner)
            copy.start()
            pair[slot, half] = copy
    for half in range(halves):
        for slot, place in enumerate(order[:-1]):
            pair[slot, half].wait_recv()
            added = part_ref[place, core, half].astype(jnp.float32) + near_ref[slot, half].astype(jnp.float32)
            sum_ref[slot, half] = added.astype(jnp.bfloat16)
            copy = remote(sum_ref.at[slot, half], far_ref.at[slot, half], far_send.at[slot, half], far_recv.at[slot, half], "tensor", peers[slot])
            copy.start()
            far[slot, half] = copy
    for half in range(halves):
        pair[chips - 1, half].wait_recv()
        shared = part_ref[chip, core, half].astype(jnp.float32) + near_ref[chips - 1, half].astype(jnp.float32)
        for slot in range(chips - 1):
            far[slot, half].wait_recv()
            shared = shared + far_ref[slot, half].astype(jnp.float32)
        squares = jnp.mean(shared * shared, axis=1, keepdims=True)
        own_ref[half] = (shared * lax.rsqrt(squares + SCALE_EPS) * gain_ref[...]).astype(jnp.bfloat16)
        landing = all_ref.at[chip, core, half]
        for slot in range(chips - 1):
            copy = remote(own_ref.at[half], landing, out_send.at[slot, half], out_recv.at[slot, half], "tensor", peers[slot])
            copy.start()
            outward[slot, half] = copy
        copy = remote(own_ref.at[half], landing, back_send.at[chips - 1, half], back_recv.at[chips - 1, half], "tensor", partner)
        copy.start()
        home[half] = copy
        all_ref[chip, core, half] = own_ref[half]
    columns = all_ref.shape[4]

    def finish(place):
        gathered = all_ref[place].reshape(2 * halves * rows, columns)
        out_ref[place] = dot(gathered, mixer_ref[...]).astype(jnp.bfloat16)

    def origin(slot):
        return lax.rem(chip + chips - 1 - slot, chips)

    def close(slot):
        for half in range(halves):
            back[slot, half].wait_recv()
        finish(origin(slot))

    for half in range(halves):
        home[half].wait_recv()
    finish(chip)
    for half in range(halves):
        for slot in range(chips - 1):
            outward[slot, half].wait_recv()
            block = all_ref.at[origin(slot), core, half]
            copy = remote(block, block, back_send.at[slot, half], back_recv.at[slot, half], "tensor", partner)
            copy.start()
            back[slot, half] = copy
            if slot and half == halves - 1:
                close(slot - 1)
    close(chips - 2)
    for copies in (pair, far, outward, home, back):
        for copy in copies.values():
            copy.wait_send()


def layer(tokens, retain, norm_gain, norm_bias, rate, angle, source, output, skip, weight, gain, mixer):
    length, channels = tokens.shape
    ndim = rate.shape[0]
    blocks = length // STEPS
    count = lax.axis_size("span")
    chips = lax.axis_size("tensor") // 2
    rows, columns = length // (2 * chips), weight.shape[1]
    halves = 2 if rows % 32 == 0 else 1
    block = (halves, rows // halves, columns)
    f32, bf16 = jnp.float32, jnp.bfloat16
    sems = pltpu.SemaphoreType.DMA
    hbm = pl.BlockSpec(memory_space=pltpu.HBM)
    out = pl.pallas_call(
        functools.partial(layer_kernel, count, chips),
        out_shape=jax.ShapeDtypeStruct((chips, 2 * rows, mixer.shape[1]), bf16),
        in_specs=[VMEM] * 10 + [hbm, hbm],
        out_specs=VMEM,
        scratch_shapes=[
            pltpu.VMEM(weight.shape, bf16),
            pltpu.VMEM(mixer.shape, bf16),
            pltpu.VMEM((8, channels), f32),
            pltpu.VMEM((count, 8, channels), f32),
            pltpu.VMEM((8, channels), f32),
            pltpu.VMEM((length, channels), f32),
            pltpu.VMEM((length, channels), f32),
            pltpu.VMEM((length, LANES), f32),
            pltpu.VMEM((2, STEPS + 1, ndim, channels), f32),
            pltpu.VMEM((2, ndim, channels), f32),
            pltpu.VMEM((2, ndim, STEPS, channels), f32),
            pltpu.VMEM((2, blocks + 1, ndim, channels), f32),
            pltpu.VMEM((2 * ndim, channels), bf16),
            pltpu.VMEM((count, 2 * ndim, channels), bf16),
            pltpu.VMEM((8, LANES), f32),
            pltpu.VMEM((count, 8, LANES), f32),
            pltpu.VMEM((length, channels), f32),
            pltpu.VMEM((chips, 2) + block, bf16),
            pltpu.VMEM((chips,) + block, bf16),
            pltpu.VMEM((chips - 1,) + block, bf16),
            pltpu.VMEM((chips - 1,) + block, bf16),
            pltpu.VMEM(block, bf16),
            pltpu.VMEM((chips, 2) + block, bf16),
            sems((2,)),
            sems((1, count - 1)),
            sems((1, count - 1)),
            sems((2, count - 1)),
            sems((2, count - 1)),
            sems((chips, halves)),
            sems((chips, halves)),
            sems((chips - 1, halves)),
            sems((chips - 1, halves)),
            sems((chips - 1, halves)),
            sems((chips - 1, halves)),
            sems((chips, halves)),
            sems((chips, halves)),
        ],
        compiler_params=pltpu.CompilerParams(collective_id=0, has_side_effects=True),
        name="layer",
    )(
        tokens,
        retain.reshape(1, -1),
        norm_gain.reshape(1, -1),
        norm_bias.reshape(1, -1),
        rate,
        angle,
        source,
        output,
        skip.reshape(1, -1),
        gain.reshape(1, -1),
        weight,
        mixer,
    )
    return out.reshape(length, mixer.shape[1])


def solution(mesh):
    in_specs = (
        P("span", "tensor"),
        P("span"),
        P("tensor"),
        P("tensor"),
        P(None, "tensor"),
        P(None, "tensor"),
        P(None, "tensor"),
        P(None, None, "tensor"),
        P("tensor"),
        P("tensor", None),
        P(),
        P(None, "tensor"),
    )
    return jax.shard_map(layer, mesh=mesh, in_specs=in_specs, out_specs=P("span", "tensor"), check_vma=False)
```

profile of v0, /device:TPU:7, one launch (start us, length us, event | category | flops | bytes accessed | tf_op | source)
XLA Modules:
  0.0 34.4 jit_solution(10394980867672707252)
XLA Ops:
  0.0 32.7 %layer.1 = bf16[4,64,512]{2,1,0:T(8,128)(2,1)} custom-call(bf16[256,512]{1,0:T(8,128)(2,1)} %tokens_ref.1, f32[1,256]{1,0:T(1,128)} %bitcast.11, f32[1,512]{1,0:T(1,128)} %bitcast.8, f32[1,512]{1,0:T(1,128)} %bitcast.9, f32[16,512]{1,0:T(8,128)} %rate_ref.1, f32[16,512]{1,0:T(8,128)} %angle_ref.1, f32[16,512]{1,0:T(8,128)} %input_ref.1, ...), custom_call_target="tpu_custom_call" | custom-call | tf_op jit(solution)/shard_map/layer/pallas_call | solution.py:403
  32.7 1.7 %copy.14 = bf16[256,512]{1,0:T(8,128)(2,1)} copy(bf16[256,512]{1,0:T(8,128)(2,1)} %bitcast.6) | data formatting | bytes 524288
where the time goes:
time: 34.5 us; the launch traced here: 34.4 us
  Pallas kernels  32.7 us (95%)
  local copies, waits for them, and re-layouts  1.67 us (5%)
    pallas_call x1, Pallas kernels, layer(): pl.pallas_call(functools.partial(layer_kernel, count, chips), out_shape=j...  32.7 us
    unnamed x1, local copies, waits for them, and re-layouts  1.67 us

commit v1 on v0

v1 whole, which is shorter than its diff:
```python
import functools

import jax
import jax.numpy as jnp
from jax import lax
from jax.experimental import pallas as pl
from jax.experimental.pallas import tpu as pltpu
from jax.sharding import PartitionSpec as P

GROUP = 64
STEPS = 8
LANES = 128
ROWS = 32
ENTER = 256
LEAVE = 256
NORM_EPS = 1e-05
SCALE_EPS = 1e-06

MESH = pl.DeviceIdType.MESH
VMEM = pl.BlockSpec(memory_space=pltpu.VMEM)


def dot(a, b):
    return jnp.dot(a, b, preferred_element_type=jnp.float32)


def pieces(values, count):
    out = []
    for _ in range(count):
        piece = values.astype(jnp.bfloat16)
        out.append(piece)
        values = values - piece.astype(jnp.float32)
    return out


def group_ones(channels):
    row = lax.broadcasted_iota(jnp.int32, (channels, channels), 0) // GROUP
    column = lax.broadcasted_iota(jnp.int32, (channels, channels), 1) // GROUP
    return (row == column).astype(jnp.bfloat16)


def remote(source, target, send_sem, recv_sem, axis, device):
    return pltpu.make_async_remote_copy(
        src_ref=source,
        dst_ref=target,
        send_sem=send_sem,
        recv_sem=recv_sem,
        device_id={axis: device},
        device_id_type=MESH,
    )


def to_later(count, pairs, send_sem, recv_sem):
    me = lax.axis_index("span")
    for step in range(1, count):

        @pl.when(me + step < count)
        def _():
            for item, (source, landing) in enumerate(pairs):
                remote(source, landing.at[me], send_sem.at[item, step - 1], recv_sem.at[item, step - 1], "span", me + step).start()


def from_earlier(count, pairs, send_sem, recv_sem):
    me = lax.axis_index("span")
    for step in range(1, count):

        @pl.when(me >= step)
        def _():
            for item, (source, landing) in enumerate(pairs):
                remote(source, landing.at[me], send_sem.at[item, step - 1], recv_sem.at[item, step - 1], "span", me - step).wait_recv()


def sent_later(count, pairs, send_sem, recv_sem):
    me = lax.axis_index("span")
    for step in range(1, count):

        @pl.when(me + step < count)
        def _():
            for item, (source, landing) in enumerate(pairs):
                remote(source, landing.at[me], send_sem.at[item, step - 1], recv_sem.at[item, step - 1], "span", me + step).wait_send()


def wide(column, width):
    return jnp.concatenate([column] * (width // LANES), axis=1)


def lanes_of(channels, width):
    return [slice(start, start + width) for start in range(0, channels, width)]


def layer_kernel(
    count,
    chips,
    tokens_hbm,
    retain_hbm,
    norm_gain_hbm,
    bias_hbm,
    rate_hbm,
    angle_hbm,
    input_hbm,
    output_hbm,
    skip_hbm,
    gain_hbm,
    weight_hbm,
    mixer_hbm,
    out_ref,
    tokens_ref,
    retain_ref,
    norm_gain_ref,
    bias_ref,
    rate_ref,
    angle_ref,
    input_ref,
    output_ref,
    skip_ref,
    gain_ref,
    weight_ref,
    mixer_ref,
    total_ref,
    totals_ref,
    before_ref,
    normed_ref,
    scaled_ref,
    prefix_ref,
    power_ref,
    unit_ref,
    whole_ref,
    carry_ref,
    read_ref,
    start_ref,
    state_ref,
    states_ref,
    kept_ref,
    kepts_ref,
    ema_ref,
    active_ref,
    mate_ref,
    part_ref,
    hop_ref,
    land_ref,
    all_ref,
    load_sem,
    total_send,
    total_recv,
    kept_send,
    kept_recv,
    state_send,
    state_recv,
    weight_send,
    weight_recv,
    mate_send,
    mate_recv,
    hop_send,
    hop_recv,
    home_send,
    home_recv,
):
    length, channels = tokens_ref.shape
    ndim = rate_ref.shape[0]
    blocks = length // STEPS
    pairs, _, rows, columns = all_ref.shape
    span = lax.axis_index("span")
    me = lax.axis_index("tensor")
    core = lax.rem(me, 2)
    chip = lax.div(me, 2)
    partner = me + 1 - 2 * core
    left, right = chip > 0, chip < chips - 1
    near = jnp.where(2 * chip < chips, 0, 1)
    far = 1 - near
    inner, outer = me + 2 - 4 * near, me - 2 + 4 * near
    end = jnp.logical_or(chip == 0, chip == chips - 1)

    barrier = pltpu.get_barrier_semaphore()
    for step in range(1, count):
        pl.semaphore_signal(barrier, inc=1, device_id={"span": lax.rem(span + step, count)}, device_id_type=MESH)
    pl.semaphore_signal(barrier, inc=1, device_id={"tensor": partner}, device_id_type=MESH)

    @pl.when(left)
    def _():
        pl.semaphore_signal(barrier, inc=1, device_id={"tensor": me - 2}, device_id_type=MESH)

    @pl.when(right)
    def _():
        pl.semaphore_signal(barrier, inc=1, device_id={"tensor": me + 2}, device_id_type=MESH)

    moves = [
        (tokens_hbm, tokens_ref),
        (rate_hbm, rate_ref),
        (angle_hbm, angle_ref),
        (input_hbm, input_ref),
        (output_hbm, output_ref),
        (retain_hbm, retain_ref),
        (norm_gain_hbm, norm_gain_ref),
        (bias_hbm, bias_ref),
        (skip_hbm, skip_ref),
        (gain_hbm, gain_ref),
        (weight_hbm, weight_ref.at[0]),
        (mixer_hbm, mixer_ref),
    ]
    loads = [pltpu.make_async_copy(source, target, load_sem.at[item]) for item, (source, target) in enumerate(moves)]
    for load in loads:
        load.start()

    ones = group_ones(channels)
    loads[0].wait()
    tokens = tokens_ref[...]
    values = tokens.astype(jnp.float32)
    total = jnp.sum(values, axis=0, keepdims=True)
    squares = jnp.sum(values * values, axis=0, keepdims=True)
    summed = jnp.concatenate([total, squares, jnp.zeros((6, channels), jnp.float32)], axis=0)
    total_ref[...] = sum(dot(piece, ones) for piece in pieces(summed, 3))
    pl.semaphore_wait(barrier, count + left.astype(jnp.int32) + right.astype(jnp.int32))
    stats_pairs = [(total_ref, totals_ref)]
    to_later(count, stats_pairs, total_send, total_recv)
    swap = remote(weight_hbm, weight_ref.at[1], weight_send, weight_recv, "tensor", partner)
    swap.start()

    for load in loads[1:10]:
        load.wait()
    row = lax.broadcasted_iota(jnp.int32, (length, length), 0)
    column = lax.broadcasted_iota(jnp.int32, (length, length), 1)
    diagonal = jnp.where(row == column, jnp.broadcast_to(retain_ref[...], (length, length)), 0.0)
    keep = sum(dot(piece, jnp.ones((length, LANES), jnp.bfloat16)) for piece in pieces(diagonal, 3))
    kept = keep.reshape(blocks, STEPS, LANES)
    while kept.shape[0] > 1:
        half = kept.shape[0] // 2
        kept = kept[:half] * kept[half:]
    kept = kept[0]
    for by in (1, 2, 4):
        kept = kept * pltpu.roll(kept, by, 0)
    kept_ref[...] = kept
    kept_pairs = [(kept_ref, kepts_ref)]
    to_later(count, kept_pairs, kept_send, kept_recv)

    rate, angle = rate_ref[...], angle_ref[...]
    size = jnp.exp(-rate)
    turn_re = size * jnp.cos(angle)
    turn_im = size * jnp.sin(angle)
    weight = (1.0 - size) * input_ref[...]
    read_re = weight * output_ref[0]
    read_im = weight * output_ref[1]
    power_re, power_im = jnp.ones_like(rate), jnp.zeros_like(rate)
    lag_rows = []
    for lag in range(STEPS + 1):
        if lag < STEPS:
            lag_rows.append(jnp.sum(read_re * power_re - read_im * power_im, axis=0, keepdims=True))
        power_ref[0, lag] = power_re
        power_ref[1, lag] = power_im
        power_re, power_im = power_re * turn_re - power_im * turn_im, power_re * turn_im + power_im * turn_re
    unit_ref[0] = read_re * turn_re - read_im * turn_im
    unit_ref[1] = read_re * turn_im + read_im * turn_re
    whole = jnp.exp(-rate * length)
    whole_ref[0] = whole * jnp.cos(angle * length)
    whole_ref[1] = whole * jnp.sin(angle * length)
    step_row = lax.broadcasted_iota(jnp.int32, (STEPS, channels), 0)

    def table(part, carried):
        here = pl.ds(part, 1)
        re = jnp.broadcast_to(unit_ref[0, here, :], (STEPS, channels))
        im = jnp.broadcast_to(unit_ref[1, here, :], (STEPS, channels))
        for bit in (1, 2, 4):
            chosen = (step_row // bit) % 2 == 1
            by_re = jnp.where(chosen, jnp.broadcast_to(power_ref[0, bit, here, :], (STEPS, channels)), 1.0)
            by_im = jnp.where(chosen, jnp.broadcast_to(power_ref[1, bit, here, :], (STEPS, channels)), 0.0)
            re, im = re * by_re - im * by_im, re * by_im + im * by_re
        read_ref[0, part] = re
        read_ref[1, part] = im
        return carried

    lax.fori_loop(0, ndim, table, 0)

    sums = dot(tokens, ones)
    squares = sum(dot(piece, ones) for piece in pieces(values * values, 2))
    lower = (column <= row).astype(jnp.bfloat16)
    cum_sum = sum(dot(lower, piece) for piece in pieces(sums, 3))
    cum_sq = sum(dot(lower, piece) for piece in pieces(squares, 3))
    place_in = lax.broadcasted_iota(jnp.int32, (length, LANES), 0) % STEPS
    prefix = keep
    suffix = jnp.where(place_in < STEPS - 1, pltpu.roll(keep, length - 1, 0), 1.0)
    for by in (1, 2, 4):
        prefix = jnp.where(place_in >= by, prefix * pltpu.roll(prefix, by, 0), prefix)
        suffix = jnp.where(place_in + by < STEPS, suffix * pltpu.roll(suffix, length - by, 0), suffix)
    prefix_ref[...] = prefix
    position = lax.broadcasted_iota(jnp.int32, (length, LANES), 0)
    share = wide(1.0 / ((span * length + position + 1) * GROUP).astype(jnp.float32), channels)

    from_earlier(count, stats_pairs, total_send, total_recv)
    before_ref[...] = jnp.zeros((8, channels), jnp.float32)
    for other in range(count - 1):

        @pl.when(other < span)
        def _():
            before_ref[...] += totals_ref[other]

    average = (before_ref[0:1] + cum_sum) * share
    spread = (before_ref[1:2] + cum_sq) * share - average * average
    inverse = lax.rsqrt(spread + NORM_EPS)
    normed = (values - average) * inverse * norm_gain_ref[...] + bias_ref[...]
    normed_ref[...] = normed
    scaled_ref[...] = normed * wide(suffix, channels)

    width = min(ENTER, channels)
    for lanes in lanes_of(channels, width):
        whole_re, whole_im = power_ref[0, STEPS, :, lanes], power_ref[1, STEPS, :, lanes]

        def enter(block, carried):
            re, im = carried
            start_ref[0, block, :, lanes] = re
            start_ref[1, block, :, lanes] = im
            first = pl.multiple_of(block * STEPS, STEPS)
            factor = wide(prefix_ref[pl.ds(first + STEPS - 1, 1), :], width)
            add_re = jnp.broadcast_to(scaled_ref[pl.ds(first + STEPS - 1, 1), lanes], (ndim, width))
            add_im = jnp.zeros((ndim, width), jnp.float32)
            for step in range(STEPS - 1):
                entry = scaled_ref[pl.ds(first + step, 1), lanes]
                lag = STEPS - 1 - step
                add_re = add_re + power_ref[0, lag, :, lanes] * entry
                add_im = add_im + power_ref[1, lag, :, lanes] * entry
            next_re = (whole_re * re - whole_im * im) * factor + add_re
            next_im = (whole_re * im + whole_im * re) * factor + add_im
            return next_re, next_im

        zero = jnp.zeros((ndim, width), jnp.float32)
        re, im = lax.fori_loop(0, blocks, enter, (zero, zero))
        state_ref[0:ndim, lanes] = re.astype(state_ref.dtype)
        state_ref[ndim : 2 * ndim, lanes] = im.astype(state_ref.dtype)
    state_pairs = [(state_ref, states_ref)]
    to_later(count, state_pairs, state_send, state_recv)

    for lanes in lanes_of(channels, LANES):
        reach = jnp.where(place_in >= 0, 1.0, 0.0)
        here = normed_ref[:, lanes]
        within = here * lag_rows[0][:, lanes]
        for lag in range(1, STEPS):
            reach = jnp.where(place_in >= lag, reach * (pltpu.roll(keep, lag - 1, 0) if lag > 1 else keep), 0.0)
            within = within + pltpu.roll(here, lag, 0) * (lag_rows[lag][:, lanes] * reach)
        ema_ref[:, lanes] = within + skip_ref[:, lanes] * here

    @pl.when(end)
    def _():
        land_ref[near] = jnp.zeros(land_ref.shape[1:], land_ref.dtype)

    loads[10].wait()
    loads[11].wait()
    swap.wait_recv()
    from_earlier(count, kept_pairs, kept_send, kept_recv)
    carry_ref[...] = jnp.zeros(carry_ref.shape, jnp.float32)
    from_earlier(count, state_pairs, state_send, state_recv)
    for other in range(count - 1):

        @pl.when(other < span)
        def _():
            kept = wide(kepts_ref[other, 0:1, :], channels)
            re, im = carry_ref[0], carry_ref[1]
            by_re, by_im = whole_ref[0], whole_ref[1]
            carry_ref[0] = (by_re * re - by_im * im) * kept + states_ref[other, 0:ndim].astype(jnp.float32)
            carry_ref[1] = (by_re * im + by_im * re) * kept + states_ref[other, ndim : 2 * ndim].astype(jnp.float32)

    width = min(LEAVE, channels)
    inside = rows // STEPS

    def produce(pair, side):
        chunk = 2 * pair + side
        for lanes in lanes_of(channels, width):
            whole_re, whole_im = power_ref[0, STEPS, :, lanes], power_ref[1, STEPS, :, lanes]
            re, im = carry_ref[0, :, lanes], carry_ref[1, :, lanes]
            for block in range(chunk * inside, (chunk + 1) * inside):
                start_ref[0, block, :, lanes] += re
                start_ref[1, block, :, lanes] += im
                factor = wide(prefix_ref[block * STEPS + STEPS - 1 : block * STEPS + STEPS, :], width)
                re, im = (whole_re * re - whole_im * im) * factor, (whole_re * im + whole_im * re) * factor
            carry_ref[0, :, lanes] = re
            carry_ref[1, :, lanes] = im
            reads = [None] * inside
            for part in range(ndim):
                by_re, by_im = read_ref[0, part, :, lanes], read_ref[1, part, :, lanes]
                for spot in range(inside):
                    block = chunk * inside + spot
                    term = by_re * start_ref[0, block, part : part + 1, lanes] - by_im * start_ref[1, block, part : part + 1, lanes]
                    reads[spot] = term if reads[spot] is None else reads[spot] + term
            for spot in range(inside):
                here = slice((chunk * inside + spot) * STEPS, (chunk * inside + spot + 1) * STEPS)
                ema_ref[here, lanes] += reads[spot] * wide(prefix_ref[here, :], width)
        ema = ema_ref[chunk * rows : (chunk + 1) * rows, :]
        active_ref[pair, side] = (ema / (1.0 + jnp.exp(-ema))).astype(jnp.bfloat16)

        @pl.when(core != side)
        def _():
            remote(active_ref.at[pair, side], mate_ref.at[pair], mate_send.at[pair], mate_recv.at[pair], "tensor", partner).start()

    def hop(way, pair, target):
        return remote(hop_ref.at[way, pair], land_ref.at[way, pair], hop_send.at[way, pair], hop_recv.at[way, pair], "tensor", target)

    def mated(pair):
        return remote(active_ref.at[pair, 1 - core], mate_ref.at[pair], mate_send.at[pair], mate_recv.at[pair], "tensor", partner)

    def multiply(pair):
        mated(pair).wait_recv()
        product = dot(active_ref[pair, core], weight_ref[0]) + dot(mate_ref[pair], weight_ref[1])
        part_ref[pair] = product

        @pl.when(end)
        def _():
            hop_ref[near, pair] = product.astype(jnp.bfloat16)
            hop(near, pair, inner).start()

    for pair in range(pairs):
        produce(pair, 0)
        produce(pair, 1)
        if pair:
            multiply(pair - 1)
    multiply(pairs - 1)

    @pl.when(jnp.logical_not(end))
    def _():
        for pair in range(pairs):
            hop(near, pair, inner).wait_recv()
            hop_ref[near, pair] = (part_ref[pair] + land_ref[near, pair].astype(jnp.float32)).astype(jnp.bfloat16)
            hop(near, pair, inner).start()

    def home(pair):
        slot = all_ref.at[pair, core]
        return remote(slot, slot, home_send.at[pair], home_recv.at[pair], "tensor", partner)

    def finish(pair):
        home(pair).wait_recv()
        gathered = all_ref[pair].reshape(2 * rows, columns)
        out_ref[2 * pair * rows : 2 * (pair + 1) * rows, :] = dot(gathered, mixer_ref[...]).astype(jnp.bfloat16)

    for pair in range(pairs):
        hop(far, pair, outer).wait_recv()
        running = part_ref[pair] + land_ref[far, pair].astype(jnp.float32)

        @pl.when(jnp.logical_not(end))
        def _():
            hop_ref[far, pair] = running.astype(jnp.bfloat16)
            hop(far, pair, outer).start()

        shared = running + land_ref[near, pair].astype(jnp.float32)
        squares = jnp.mean(shared * shared, axis=1, keepdims=True)
        all_ref[pair, core] = (shared * lax.rsqrt(squares + SCALE_EPS) * gain_ref[...]).astype(jnp.bfloat16)
        home(pair).start()
        if pair:
            finish(pair - 1)
    finish(pairs - 1)

    sent_later(count, stats_pairs, total_send, total_recv)
    sent_later(count, kept_pairs, kept_send, kept_recv)
    sent_later(count, state_pairs, state_send, state_recv)
    swap.wait_send()
    for pair in range(pairs):
        mated(pair).wait_send()
        home(pair).wait_send()
        hop(near, pair, inner).wait_send()

    @pl.when(jnp.logical_not(end))
    def _():
        for pair in range(pairs):
            hop(far, pair, outer).wait_send()


def layer(tokens, retain, norm_gain, norm_bias, rate, angle, source, output, skip, weight, gain, mixer):
    length, channels = tokens.shape
    ndim = rate.shape[0]
    blocks = length // STEPS
    count = lax.axis_size("span")
    chips = lax.axis_size("tensor") // 2
    columns = weight.shape[1]
    pairs = length // (2 * ROWS)
    f32, bf16 = jnp.float32, jnp.bfloat16
    sems = pltpu.SemaphoreType.DMA
    hbm = pl.BlockSpec(memory_space=pltpu.HBM)
    operands = [
        tokens,
        retain.reshape(1, -1),
        norm_gain.reshape(1, -1),
        norm_bias.reshape(1, -1),
        rate,
        angle,
        source,
        output,
        skip.reshape(1, -1),
        gain.reshape(1, -1),
        weight,
        mixer,
    ]
    held = [pltpu.VMEM(a.shape, a.dtype) for a in operands[:10]]
    return pl.pallas_call(
        functools.partial(layer_kernel, count, chips),
        out_shape=pltpu.VMEM((length, mixer.shape[1]), bf16),
        in_specs=[hbm] * 12,
        out_specs=VMEM,
        scratch_shapes=held
        + [
            pltpu.VMEM((2,) + weight.shape, bf16),
            pltpu.VMEM(mixer.shape, bf16),
            pltpu.VMEM((8, channels), f32),
            pltpu.VMEM((count, 8, channels), f32),
            pltpu.VMEM((8, channels), f32),
            pltpu.VMEM((length, channels), f32),
            pltpu.VMEM((length, channels), f32),
            pltpu.VMEM((length, LANES), f32),
            pltpu.VMEM((2, STEPS + 1, ndim, channels), f32),
            pltpu.VMEM((2, ndim, channels), f32),
            pltpu.VMEM((2, ndim, channels), f32),
            pltpu.VMEM((2, ndim, channels), f32),
            pltpu.VMEM((2, ndim, STEPS, channels), f32),
            pltpu.VMEM((2, blocks, ndim, channels), f32),
            pltpu.VMEM((2 * ndim, channels), bf16),
            pltpu.VMEM((count, 2 * ndim, channels), bf16),
            pltpu.VMEM((8, LANES), f32),
            pltpu.VMEM((count, 8, LANES), f32),
            pltpu.VMEM((length, channels), f32),
            pltpu.VMEM((pairs, 2, ROWS, channels), bf16),
            pltpu.VMEM((pairs, ROWS, channels), bf16),
            pltpu.VMEM((pairs, ROWS, columns), f32),
            pltpu.VMEM((2, pairs, ROWS, columns), bf16),
            pltpu.VMEM((2, pairs, ROWS, columns), bf16),
            pltpu.VMEM((pairs, 2, ROWS, columns), bf16),
            sems((12,)),
            sems((1, count - 1)),
            sems((1, count - 1)),
            sems((1, count - 1)),
            sems((1, count - 1)),
            sems((1, count - 1)),
            sems((1, count - 1)),
            sems(()),
            sems(()),
            sems((pairs,)),
            sems((pairs,)),
            sems((2, pairs)),
            sems((2, pairs)),
            sems((pairs,)),
            sems((pairs,)),
        ],
        compiler_params=pltpu.CompilerParams(collective_id=0, has_side_effects=True),
        name="layer",
    )(*operands)


def solution(mesh):
    in_specs = (
        P("span", "tensor"),
        P("span"),
        P("tensor"),
        P("tensor"),
        P(None, "tensor"),
        P(None, "tensor"),
        P(None, "tensor"),
        P(None, None, "tensor"),
        P("tensor"),
        P("tensor", None),
        P(),
        P(None, "tensor"),
    )
    return jax.shard_map(layer, mesh=mesh, in_specs=in_specs, out_specs=P("span", "tensor"), check_vma=False)
```

time: 34.5 us -> 31.7 us (0.919)
  the two profiles are of different devices: /device:TPU:7 before, /device:TPU:5 now
where the time goes in v1:
time: 31.7 us; the launch traced here: 31.5 us
  Pallas kernels  30.8 us (97%)
  local copies, waits for them, and re-layouts  0.71 us (2%)
    pallas_call x1, Pallas kernels, layer(): pl.pallas_call(functools.partial(layer_kernel, count, chips), out_shape=p...  30.8 us
    unnamed x1, local copies, waits for them, and re-layouts  0.71 us

profile of v1, /device:TPU:5, one launch (start us, length us, event | category | flops | bytes accessed | tf_op | source)
XLA Modules:
  0.0 31.5 jit_solution(10074943964674548976)
XLA Ops:
  0.0 30.8 %layer.1 = bf16[256,512]{1,0:T(8,128)(2,1)S(1)} custom-call(bf16[256,512]{1,0:T(8,128)(2,1)} %tokens_hbm.1, f32[1,256]{1,0:T(1,128)} %bitcast.9, f32[1,512]{1,0:T(1,128)} %bitcast.6, f32[1,512]{1,0:T(1,128)} %bitcast.7, f32[16,512]{1,0:T(8,128)} %rate_hbm.1, f32[16,512]{1,0:T(8,128)} %angle_hbm.1, f32[16,512]{1,0:T(8,128)} %input_hbm.1, ...), custom_call_target="tpu_custom_call" | custom-call | tf_op jit(solution)/shard_map/layer/pallas_call | solution.py:488
  30.8 0.7 %copy.14 = bf16[256,512]{1,0:T(8,128)(2,1)} copy(bf16[256,512]{1,0:T(8,128)(2,1)S(1)} %layer.1) | data formatting | bytes 524288

commit v2 on v1

--- a/solution.py
+++ b/solution.py
@@ -11,7 +11,10 @@
 STEPS = 8
 LANES = 128
 ROWS = 32
-ENTER = 256
+FINE = 16
+LAG = 5
+ENTER = 128
+UNROLL = 4
 LEAVE = 256
 NORM_EPS = 1e-05
 SCALE_EPS = 1e-06
@@ -50,34 +53,35 @@
     )
 
 
-def to_later(count, pairs, send_sem, recv_sem):
+def to_span(source, landing, send_sem, recv_sem, step, place, device):
+    return remote(source, landing.at[place], send_sem, recv_sem.at[step - 1], "span", device)
+
+
+def to_later(count, source, landing, send_sem, recv_sem):
     me = lax.axis_index("span")
     for step in range(1, count):
 
         @pl.when(me + step < count)
         def _():
-            for item, (source, landing) in enumerate(pairs):
-                remote(source, landing.at[me], send_sem.at[item, step - 1], recv_sem.at[item, step - 1], "span", me + step).start()
-
-
-def from_earlier(count, pairs, send_sem, recv_sem):
+            to_span(source, landing, send_sem, recv_sem, step, me, me + step).start()
+
+
+def from_earlier(count, source, landing, send_sem, recv_sem):
     me = lax.axis_index("span")
     for step in range(1, count):
 
         @pl.when(me >= step)
         def _():
-            for item, (source, landing) in enumerate(pairs):
-                remote(source, landing.at[me], send_sem.at[item, step - 1], recv_sem.at[item, step - 1], "span", me - step).wait_recv()
-
-
-def sent_later(count, pairs, send_sem, recv_sem):
+            to_span(source, landing, send_sem, recv_sem, step, me, me - step).wait_recv()
+
+
+def sent_later(count, source, landing, send_sem, recv_sem):
     me = lax.axis_index("span")
     for step in range(1, count):
 
         @pl.when(me + step < count)
         def _():
-            for item, (source, landing) in enumerate(pairs):
-                remote(source, landing.at[me], send_sem.at[item, step - 1], recv_sem.at[item, step - 1], "span", me + step).wait_send()
+            to_span(source, landing, send_sem, recv_sem, step, me, me + step).wait_send()
 
 
 def wide(column, width):
@@ -130,8 +134,6 @@
     start_ref,
     state_ref,
     states_ref,
-    kept_ref,
-    kepts_ref,
     ema_ref,
     active_ref,
     mate_ref,
@@ -142,8 +144,6 @@
     load_sem,
     total_send,
     total_recv,
-    kept_send,
-    kept_recv,
     state_send,
     state_recv,
     weight_send,
@@ -158,7 +158,9 @@
     length, channels = tokens_ref.shape
     ndim = rate_ref.shape[0]
     blocks = length // STEPS
-    pairs, _, rows, columns = all_ref.shape
+    pairs, _, subs, fine, columns = all_ref.shape
+    rows = subs * fine
+    count_of = pairs * subs
     span = lax.axis_index("span")
     me = lax.axis_index("tensor")
     core = lax.rem(me, 2)
@@ -184,41 +186,27 @@
         pl.semaphore_signal(barrier, inc=1, device_id={"tensor": me + 2}, device_id_type=MESH)
 
     moves = [
-        (tokens_hbm, tokens_ref),
-        (rate_hbm, rate_ref),
-        (angle_hbm, angle_ref),
-        (input_hbm, input_ref),
-        (output_hbm, output_ref),
-        (retain_hbm, retain_ref),
-        (norm_gain_hbm, norm_gain_ref),
-        (bias_hbm, bias_ref),
-        (skip_hbm, skip_ref),
-        (gain_hbm, gain_ref),
-        (weight_hbm, weight_ref.at[0]),
-        (mixer_hbm, mixer_ref),
+        (retain_hbm, retain_ref, 0),
+        (tokens_hbm, tokens_ref, 1),
+        (rate_hbm, rate_ref, 2),
+        (angle_hbm, angle_ref, 2),
+        (input_hbm, input_ref, 2),
+        (output_hbm, output_ref, 2),
+        (norm_gain_hbm, norm_gain_ref, 2),
+        (bias_hbm, bias_ref, 2),
+        (skip_hbm, skip_ref, 2),
+        (gain_hbm, gain_ref, 2),
+        (weight_hbm, weight_ref.at[0], 3),
+        (mixer_hbm, mixer_ref, 3),
     ]
-    loads = [pltpu.make_async_copy(source, target, load_sem.at[item]) for item, (source, target) in enumerate(moves)]
+    loads = [pltpu.make_async_copy(source, target, load_sem.at[item]) for source, target, item in moves]
     for load in loads:
         load.start()
 
+    row = lax.broadcasted_iota(jnp.int32, (length, length), 0)
+    column = lax.broadcasted_iota(jnp.int32, (length, length), 1)
     ones = group_ones(channels)
     loads[0].wait()
-    tokens = tokens_ref[...]
-    values = tokens.astype(jnp.float32)
-    total = jnp.sum(values, axis=0, keepdims=True)
-    squares = jnp.sum(values * values, axis=0, keepdims=True)
-    summed = jnp.concatenate([total, squares, jnp.zeros((6, channels), jnp.float32)], axis=0)
-    total_ref[...] = sum(dot(piece, ones) for piece in pieces(summed, 3))
-    pl.semaphore_wait(barrier, count + left.astype(jnp.int32) + right.astype(jnp.int32))
-    stats_pairs = [(total_ref, totals_ref)]
-    to_later(count, stats_pairs, total_send, total_recv)
-    swap = remote(weight_hbm, weight_ref.at[1], weight_send, weight_recv, "tensor", partner)
-    swap.start()
-
-    for load in loads[1:10]:
-        load.wait()
-    row = lax.broadcasted_iota(jnp.int32, (length, length), 0)
-    column = lax.broadcasted_iota(jnp.int32, (length, length), 1)
     diagonal = jnp.where(row == column, jnp.broadcast_to(retain_ref[...], (length, length)), 0.0)
     keep = sum(dot(piece, jnp.ones((length, LANES), jnp.bfloat16)) for piece in pieces(diagonal, 3))
     kept = keep.reshape(blocks, STEPS, LANES)
@@ -228,10 +216,23 @@
     kept = kept[0]
     for by in (1, 2, 4):
         kept = kept * pltpu.roll(kept, by, 0)
-    kept_ref[...] = kept
-    kept_pairs = [(kept_ref, kepts_ref)]
-    to_later(count, kept_pairs, kept_send, kept_recv)
-
+    loads[1].wait()
+    tokens = tokens_ref[...]
+    values = tokens.astype(jnp.float32)
+    total = jnp.sum(values, axis=0, keepdims=True)
+    squares = jnp.sum(values * values, axis=0, keepdims=True)
+    summed = jnp.concatenate([total, squares, jnp.zeros((6, channels), jnp.float32)], axis=0)
+    summed = sum(dot(piece, ones) for piece in pieces(summed, 3))
+    top = lax.broadcasted_iota(jnp.int32, (8, channels), 0) < 2
+    total_ref[...] = jnp.where(top, summed, wide(kept, channels))
+    pl.semaphore_wait(barrier, count + left.astype(jnp.int32) + right.astype(jnp.int32))
+    stats = (total_ref, totals_ref, total_send, total_recv)
+    to_later(count, *stats)
+    swap = remote(weight_hbm, weight_ref.at[1], weight_send, weight_recv, "tensor", partner)
+    swap.start()
+
+    for load in loads[2:10]:
+        load.wait()
     rate, angle = rate_ref[...], angle_ref[...]
     size = jnp.exp(-rate)
     turn_re = size * jnp.cos(angle)
@@ -280,11 +281,11 @@
     for by in (1, 2, 4):
         prefix = jnp.where(place_in >= by, prefix * pltpu.roll(prefix, by, 0), prefix)
         suffix = jnp.where(place_in + by < STEPS, suffix * pltpu.roll(suffix, length - by, 0), suffix)
-    prefix_ref[...] = prefix
+    prefix_ref[...] = prefix.reshape(blocks, STEPS, LANES)
     position = lax.broadcasted_iota(jnp.int32, (length, LANES), 0)
     share = wide(1.0 / ((span * length + position + 1) * GROUP).astype(jnp.float32), channels)
 
-    from_earlier(count, stats_pairs, total_send, total_recv)
+    from_earlier(count, *stats)
     before_ref[...] = jnp.zeros((8, channels), jnp.float32)
     for other in range(count - 1):
 
@@ -297,35 +298,34 @@
     inverse = lax.rsqrt(spread + NORM_EPS)
     normed = (values - average) * inverse * norm_gain_ref[...] + bias_ref[...]
     normed_ref[...] = normed
-    scaled_ref[...] = normed * wide(suffix, channels)
+    scaled_ref[...] = (normed * wide(suffix, channels)).reshape(blocks, STEPS, channels)
 
     width = min(ENTER, channels)
     for lanes in lanes_of(channels, width):
-        whole_re, whole_im = power_ref[0, STEPS, :, lanes], power_ref[1, STEPS, :, lanes]
+        powers = [(power_ref[0, lag, :, lanes], power_ref[1, lag, :, lanes]) for lag in range(STEPS + 1)]
 
         def enter(block, carried):
             re, im = carried
             start_ref[0, block, :, lanes] = re
             start_ref[1, block, :, lanes] = im
-            first = pl.multiple_of(block * STEPS, STEPS)
-            factor = wide(prefix_ref[pl.ds(first + STEPS - 1, 1), :], width)
-            add_re = jnp.broadcast_to(scaled_ref[pl.ds(first + STEPS - 1, 1), lanes], (ndim, width))
-            add_im = jnp.zeros((ndim, width), jnp.float32)
-            for step in range(STEPS - 1):
-                entry = scaled_ref[pl.ds(first + step, 1), lanes]
-                lag = STEPS - 1 - step
-                add_re = add_re + power_ref[0, lag, :, lanes] * entry
-                add_im = add_im + power_ref[1, lag, :, lanes] * entry
-            next_re = (whole_re * re - whole_im * im) * factor + add_re
-            next_im = (whole_re * im + whole_im * re) * factor + add_im
-            return next_re, next_im
+            factor = wide(prefix_ref[block, STEPS - 1 : STEPS, :], width)
+            add_re = jnp.broadcast_to(scaled_ref[block, STEPS - 1 : STEPS, lanes], (ndim, width))
+            add_im = None
+            for step in reversed(range(STEPS - 1)):
+                entry = scaled_ref[block, step : step + 1, lanes]
+                by_re, by_im = powers[STEPS - 1 - step]
+                add_re = add_re + by_re * entry
+                add_im = by_im * entry if add_im is None else add_im + by_im * entry
+            re, im = re * factor, im * factor
+            by_re, by_im = powers[STEPS]
+            return by_re * re - by_im * im + add_re, by_re * im + by_im * re + add_im
 
         zero = jnp.zeros((ndim, width), jnp.float32)
-        re, im = lax.fori_loop(0, blocks, enter, (zero, zero))
+        re, im = lax.fori_loop(0, blocks, enter, (zero, zero), unroll=UNROLL)
         state_ref[0:ndim, lanes] = re.astype(state_ref.dtype)
         state_ref[ndim : 2 * ndim, lanes] = im.astype(state_ref.dtype)
-    state_pairs = [(state_ref, states_ref)]
-    to_later(count, state_pairs, state_send, state_recv)
+    states = (state_ref, states_ref, state_send, state_recv)
+    to_later(count, *states)
 
     for lanes in lanes_of(channels, LANES):
         reach = jnp.where(place_in >= 0, 1.0, 0.0)
@@ -343,14 +343,13 @@
     loads[10].wait()
     loads[11].wait()
     swap.wait_recv()
-    from_earlier(count, kept_pairs, kept_send, kept_recv)
     carry_ref[...] = jnp.zeros(carry_ref.shape, jnp.float32)
-    from_earlier(count, state_pairs, state_send, state_recv)
+    from_earlier(count, *states)
     for other in range(count - 1):
 
         @pl.when(other < span)
         def _():
-            kept = wide(kepts_ref[other, 0:1, :], channels)
+            kept = totals_ref[other, 2:3, :]
             re, im = carry_ref[0], carry_ref[1]
             by_re, by_im = whole_ref[0], whole_ref[1]
             carry_ref[0] = (by_re * re - by_im * im) * kept + states_ref[other, 0:ndim].astype(jnp.float32)
@@ -367,7 +366,7 @@
             for block in range(chunk * inside, (chunk + 1) * inside):
                 start_ref[0, block, :, lanes] += re
                 start_ref[1, block, :, lanes] += im
-                factor = wide(prefix_ref[block * STEPS + STEPS - 1 : block * STEPS + STEPS, :], width)
+                factor = wide(prefix_ref[block, STEPS - 1 : STEPS, :], width)
                 re, im = (whole_re * re - whole_im * im) * factor, (whole_re * im + whole_im * re) * factor
             carry_ref[0, :, lanes] = re
             carry_ref[1, :, lanes] = im
@@ -380,29 +379,29 @@
                     reads[spot] = term if reads[spot] is None else reads[spot] + term
             for spot in range(inside):
                 here = slice((chunk * inside + spot) * STEPS, (chunk * inside + spot + 1) * STEPS)
-                ema_ref[here, lanes] += reads[spot] * wide(prefix_ref[here, :], width)
+                ema_ref[here, lanes] += reads[spot] * wide(prefix_ref[chunk * inside + spot], width)
         ema = ema_ref[chunk * rows : (chunk + 1) * rows, :]
         active_ref[pair, side] = (ema / (1.0 + jnp.exp(-ema))).astype(jnp.bfloat16)
 
         @pl.when(core != side)
         def _():
-            remote(active_ref.at[pair, side], mate_ref.at[pair], mate_send.at[pair], mate_recv.at[pair], "tensor", partner).start()
-
-    def hop(way, pair, target):
-        return remote(hop_ref.at[way, pair], land_ref.at[way, pair], hop_send.at[way, pair], hop_recv.at[way, pair], "tensor", target)
-
-    def mated(pair):
-        return remote(active_ref.at[pair, 1 - core], mate_ref.at[pair], mate_send.at[pair], mate_recv.at[pair], "tensor", partner)
+            remote(active_ref.at[pair, side], mate_ref.at[pair], mate_send, mate_recv.at[pair], "tensor", partner).start()
+
+    def hop(way, item, target):
+        return remote(hop_ref.at[way, item], land_ref.at[way, item], hop_send.at[way], hop_recv.at[way, item], "tensor", target)
 
     def multiply(pair):
-        mated(pair).wait_recv()
+        remote(active_ref.at[pair, 1 - core], mate_ref.at[pair], mate_send, mate_recv.at[pair], "tensor", partner).wait_recv()
         product = dot(active_ref[pair, core], weight_ref[0]) + dot(mate_ref[pair], weight_ref[1])
-        part_ref[pair] = product
+        for sub in range(subs):
+            part_ref[pair * subs + sub] = product[sub * fine : (sub + 1) * fine]
 
         @pl.when(end)
         def _():
-            hop_ref[near, pair] = product.astype(jnp.bfloat16)
-            hop(near, pair, inner).start()
+            for sub in range(subs):
+                item = pair * subs + sub
+                hop_ref[near, item] = product[sub * fine : (sub + 1) * fine].astype(jnp.bfloat16)
+                hop(near, item, inner).start()
 
     for pair in range(pairs):
         produce(pair, 0)
@@ -411,52 +410,57 @@
             multiply(pair - 1)
     multiply(pairs - 1)
 
+    def home(item):
+        slot = all_ref.at[item // subs, core, item % subs]
+        return remote(slot, slot, home_send, home_recv.at[item], "tensor", partner)
+
+    def relay(item):
+        @pl.when(jnp.logical_not(end))
+        def _():
+            hop(near, item, inner).wait_recv()
+            hop_ref[near, item] = (part_ref[item] + land_ref[near, item].astype(jnp.float32)).astype(jnp.bfloat16)
+            hop(near, item, inner).start()
+
+    def close(item):
+        hop(far, item, outer).wait_recv()
+        running = part_ref[item] + land_ref[far, item].astype(jnp.float32)
+
+        @pl.when(jnp.logical_not(end))
+        def _():
+            hop_ref[far, item] = running.astype(jnp.bfloat16)
+            hop(far, item, outer).start()
+
+        shared = running + land_ref[near, item].astype(jnp.float32)
+        squares = jnp.mean(shared * shared, axis=1, keepdims=True)
+        all_ref[item // subs, core, item % subs] = (shared * lax.rsqrt(squares + SCALE_EPS) * gain_ref[...]).astype(jnp.bfloat16)
+        home(item).start()
+
+    def finish(pair):
+        for sub in range(subs):
+            home(pair * subs + sub).wait_recv()
+        gathered = all_ref[pair].reshape(2 * rows, columns)
+        out_ref[2 * pair * rows : 2 * (pair + 1) * rows, :] = dot(gathered, mixer_ref[...]).astype(jnp.bfloat16)
+
+    for item in range(count_of + LAG):
+        if item < count_of:
+            relay(item)
+        item -= LAG
+        if item >= 0:
+            close(item)
+            if item % subs == subs - 1 and item >= subs:
+                finish(item // subs - 1)
+    finish(pairs - 1)
+
+    sent_later(count, *stats)
+    sent_later(count, *states)
+    swap.wait_send()
+    remote(mate_ref, mate_ref, mate_send, mate_recv.at[0], "tensor", partner).wait_send()
+    remote(hop_ref.at[0], land_ref.at[0], home_send, home_recv.at[0], "tensor", partner).wait_send()
+    remote(hop_ref.at[0], land_ref.at[0], hop_send.at[near], hop_recv.at[0, 0], "tensor", inner).wait_send()
+
     @pl.when(jnp.logical_not(end))
     def _():
-        for pair in range(pairs):
-            hop(near, pair, inner).wait_recv()
-            hop_ref[near, pair] = (part_ref[pair] + land_ref[near, pair].astype(jnp.float32)).astype(jnp.bfloat16)
-            hop(near, pair, inner).start()
-
-    def home(pair):
-        slot = all_ref.at[pair, core]
-        return remote(slot, slot, home_send.at[pair], home_recv.at[pair], "tensor", partner)
-
-    def finish(pair):
-        home(pair).wait_recv()
-        gathered = all_ref[pair].reshape(2 * rows, columns)
-        out_ref[2 * pair * rows : 2 * (pair + 1) * rows, :] = dot(gathered, mixer_ref[...]).astype(jnp.bfloat16)
-
-    for pair in range(pairs):
-        hop(far, pair, outer).wait_recv()
-        running = part_ref[pair] + land_ref[far, pair].astype(jnp.float32)
-
-        @pl.when(jnp.logical_not(end))
-        def _():
-            hop_ref[far, pair] = running.astype(jnp.bfloat16)
-            hop(far, pair, outer).start()
-
-        shared = running + land_ref[near, pair].astype(jnp.float32)
-        squares = jnp.mean(shared * shared, axis=1, keepdims=True)
-        all_ref[pair, core] = (shared * lax.rsqrt(squares + SCALE_EPS) * gain_ref[...]).astype(jnp.bfloat16)
-        home(pair).start()
-        if pair:
-            finish(pair - 1)
-    finish(pairs - 1)
-
-    sent_later(count, stats_pairs, total_send, total_recv)
-    sent_later(count, kept_pairs, kept_send, kept_recv)
-    sent_later(count, state_pairs, state_send, state_recv)
-    swap.wait_send()
-    for pair in range(pairs):
-        mated(pair).wait_send()
-        home(pair).wait_send()
-        hop(near, pair, inner).wait_send()
-
-    @pl.when(jnp.logical_not(end))
-    def _():
-        for pair in range(pairs):
-            hop(far, pair, outer).wait_send()
+        remote(hop_ref.at[0], land_ref.at[0], hop_send.at[far], hop_recv.at[0, 0], "tensor", outer).wait_send()
 
 
 def layer(tokens, retain, norm_gain, norm_bias, rate, angle, source, output, skip, weight, gain, mixer):
@@ -467,6 +471,7 @@
     chips = lax.axis_size("tensor") // 2
     columns = weight.shape[1]
     pairs = length // (2 * ROWS)
+    items = length // (2 * FINE)
     f32, bf16 = jnp.float32, jnp.bfloat16
     sems = pltpu.SemaphoreType.DMA
     hbm = pl.BlockSpec(memory_space=pltpu.HBM)
@@ -498,8 +503,8 @@
             pltpu.VMEM((count, 8, channels), f32),
             pltpu.VMEM((8, channels), f32),
             pltpu.VMEM((length, channels), f32),
-            pltpu.VMEM((length, channels), f32),
-            pltpu.VMEM((length, LANES), f32),
+            pltpu.VMEM((blocks, STEPS, channels), f32),
+            pltpu.VMEM((blocks, STEPS, LANES), f32),
             pltpu.VMEM((2, STEPS + 1, ndim, channels), f32),
             pltpu.VMEM((2, ndim, channels), f32),
             pltpu.VMEM((2, ndim, channels), f32),
@@ -508,30 +513,26 @@
             pltpu.VMEM((2, blocks, ndim, channels), f32),
             pltpu.VMEM((2 * ndim, channels), bf16),
             pltpu.VMEM((count, 2 * ndim, channels), bf16),
-            pltpu.VMEM((8, LANES), f32),
-            pltpu.VMEM((count, 8, LANES), f32),
             pltpu.VMEM((length, channels), f32),
             pltpu.VMEM((pairs, 2, ROWS, channels), bf16),
             pltpu.VMEM((pairs, ROWS, channels), bf16),
-            pltpu.VMEM((pairs, ROWS, columns), f32),
-            pltpu.VMEM((2, pairs, ROWS, columns), bf16),
-            pltpu.VMEM((2, pairs, ROWS, columns), bf16),
-            pltpu.VMEM((pairs, 2, ROWS, columns), bf16),
-            sems((12,)),
-            sems((1, count - 1)),
-            sems((1, count - 1)),
-            sems((1, count - 1)),
-            sems((1, count - 1)),
-            sems((1, count - 1)),
-            sems((1, count - 1)),
+            pltpu.VMEM((items, FINE, columns), f32),
+            pltpu.VMEM((2, items, FINE, columns), bf16),
+            pltpu.VMEM((2, items, FINE, columns), bf16),
+            pltpu.VMEM((pairs, 2, ROWS // FINE, FINE, columns), bf16),
+            sems((4,)),
+            sems(()),
+            sems((count - 1,)),
+            sems(()),
+            sems((count - 1,)),
+            sems(()),
             sems(()),
             sems(()),
             sems((pairs,)),
-            sems((pairs,)),
-            sems((2, pairs)),
-            sems((2, pairs)),
-            sems((pairs,)),
-            sems((pairs,)),
+            sems((2,)),
+            sems((2, items)),
+            sems(()),
+            sems((items,)),
         ],
         compiler_params=pltpu.CompilerParams(collective_id=0, has_side_effects=True),
         name="layer",

time: 31.7 us -> 30.3 us (0.956)
  Pallas kernels: 30.8 us -> 29.5 us
    pallas_call x1, Pallas kernels: 30.8 us -> 29.5 us  [layer(): pl.pallas_call(functools.partial(layer_kernel, count, chips), out_shape=p...]
where the time goes in v2:
time: 30.3 us; the launch traced here: 30.2 us
  Pallas kernels  29.5 us (97%)
  local copies, waits for them, and re-layouts  0.71 us (2%)
    pallas_call x1, Pallas kernels, layer(): pl.pallas_call(functools.partial(layer_kernel, count, chips), out_shape=p...  29.5 us
    unnamed x1, local copies, waits for them, and re-layouts  0.71 us

profile of v2, /device:TPU:5, one launch (start us, length us, event | category | flops | bytes accessed | tf_op | source)
XLA Modules:
  0.0 30.2 jit_solution(1737743580856456655)
XLA Ops:
  0.0 29.5 %layer.1 = bf16[256,512]{1,0:T(8,128)(2,1)S(1)} custom-call(bf16[256,512]{1,0:T(8,128)(2,1)} %tokens_hbm.1, f32[1,256]{1,0:T(1,128)} %bitcast.9, f32[1,512]{1,0:T(1,128)} %bitcast.6, f32[1,512]{1,0:T(1,128)} %bitcast.7, f32[16,512]{1,0:T(8,128)} %rate_hbm.1, f32[16,512]{1,0:T(8,128)} %angle_hbm.1, f32[16,512]{1,0:T(8,128)} %input_hbm.1, ...), custom_call_target="tpu_custom_call" | custom-call | tf_op jit(solution)/shard_map/layer/pallas_call | solution.py:493
  29.5 0.7 %copy.14 = bf16[256,512]{1,0:T(8,128)(2,1)} copy(bf16[256,512]{1,0:T(8,128)(2,1)S(1)} %layer.1) | data formatting | bytes 524288

commit v3 on v2

--- a/solution.py
+++ b/solution.py
@@ -13,7 +13,7 @@
 ROWS = 32
 FINE = 16
 LAG = 5
-ENTER = 128
+ENTER = 256
 UNROLL = 4
 LEAVE = 256
 NORM_EPS = 1e-05
@@ -53,26 +53,23 @@
     )
 
 
-def to_span(source, landing, send_sem, recv_sem, step, place, device):
-    return remote(source, landing.at[place], send_sem, recv_sem.at[step - 1], "span", device)
-
-
 def to_later(count, source, landing, send_sem, recv_sem):
     me = lax.axis_index("span")
     for step in range(1, count):
 
         @pl.when(me + step < count)
         def _():
-            to_span(source, landing, send_sem, recv_sem, step, me, me + step).start()
+            remote(source, landing.at[me], send_sem, recv_sem, "span", me + step).start()
 
 
 def from_earlier(count, source, landing, send_sem, recv_sem):
     me = lax.axis_index("span")
-    for step in range(1, count):
-
-        @pl.when(me >= step)
-        def _():
-            to_span(source, landing, send_sem, recv_sem, step, me, me - step).wait_recv()
+    for place in range(1, count):
+
+        @pl.when(me == place)
+        def _():
+            here = landing.at[0:place]
+            remote(here, here, send_sem, recv_sem, "span", 0).wait_recv()
 
 
 def sent_later(count, source, landing, send_sem, recv_sem):
@@ -81,7 +78,7 @@
 
         @pl.when(me + step < count)
         def _():
-            to_span(source, landing, send_sem, recv_sem, step, me, me + step).wait_send()
+            remote(source, landing.at[me], send_sem, recv_sem, "span", me + step).wait_send()
 
 
 def wide(column, width):
@@ -406,13 +403,19 @@
     for pair in range(pairs):
         produce(pair, 0)
         produce(pair, 1)
-        if pair:
-            multiply(pair - 1)
-    multiply(pairs - 1)
+
+        @pl.when(core == 0)
+        def _():
+            multiply(pair)
+
+    @pl.when(core == 1)
+    def _():
+        for pair in range(pairs):
+            multiply(pair)
 
     def home(item):
         slot = all_ref.at[item // subs, core, item % subs]
-        return remote(slot, slot, home_send, home_recv.at[item], "tensor", partner)
+        return remote(slot, slot, home_send, home_recv.at[item // subs], "tensor", partner)
 
     def relay(item):
         @pl.when(jnp.logical_not(end))
@@ -436,8 +439,8 @@
         home(item).start()
 
     def finish(pair):
-        for sub in range(subs):
-            home(pair * subs + sub).wait_recv()
+        slot = all_ref.at[pair, core]
+        remote(slot, slot, home_send, home_recv.at[pair], "tensor", partner).wait_recv()
         gathered = all_ref[pair].reshape(2 * rows, columns)
         out_ref[2 * pair * rows : 2 * (pair + 1) * rows, :] = dot(gathered, mixer_ref[...]).astype(jnp.bfloat16)
 
@@ -522,9 +525,9 @@
             pltpu.VMEM((pairs, 2, ROWS // FINE, FINE, columns), bf16),
             sems((4,)),
             sems(()),
-            sems((count - 1,)),
-            sems(()),
-            sems((count - 1,)),
+            sems(()),
+            sems(()),
+            sems(()),
             sems(()),
             sems(()),
             sems(()),
@@ -532,7 +535,7 @@
             sems((2,)),
             sems((2, items)),
             sems(()),
-            sems((items,)),
+            sems((pairs,)),
         ],
         compiler_params=pltpu.CompilerParams(collective_id=0, has_side_effects=True),
         name="layer",

time: 30.3 us -> 29.6 us (0.977)
  Pallas kernels: 29.5 us -> 28.8 us
    pallas_call x1, Pallas kernels: 29.5 us -> 28.8 us  [layer(): pl.pallas_call(functools.partial(layer_kernel, count, chips), out_shape=p...]
where the time goes in v3:
time: 29.6 us; the launch traced here: 29.5 us
  Pallas kernels  28.8 us (97%)
  local copies, waits for them, and re-layouts  0.71 us (2%)
    pallas_call x1, Pallas kernels, layer(): pl.pallas_call(functools.partial(layer_kernel, count, chips), out_shape=p...  28.8 us
    unnamed x1, local copies, waits for them, and re-layouts  0.71 us

profile of v3, /device:TPU:5, one launch (start us, length us, event | category | flops | bytes accessed | tf_op | source)
XLA Modules:
  0.0 29.5 jit_solution(17107841456829723634)
XLA Ops:
  0.0 28.8 %layer.1 = bf16[256,512]{1,0:T(8,128)(2,1)S(1)} custom-call(bf16[256,512]{1,0:T(8,128)(2,1)} %tokens_hbm.1, f32[1,256]{1,0:T(1,128)} %bitcast.9, f32[1,512]{1,0:T(1,128)} %bitcast.6, f32[1,512]{1,0:T(1,128)} %bitcast.7, f32[16,512]{1,0:T(8,128)} %rate_hbm.1, f32[16,512]{1,0:T(8,128)} %angle_hbm.1, f32[16,512]{1,0:T(8,128)} %input_hbm.1, ...), custom_call_target="tpu_custom_call" | custom-call | tf_op jit(solution)/shard_map/layer/pallas_call | solution.py:496
  28.8 0.7 %copy.14 = bf16[256,512]{1,0:T(8,128)(2,1)} copy(bf16[256,512]{1,0:T(8,128)(2,1)S(1)} %layer.1) | data formatting | bytes 524288

commit v4 on v3

--- a/solution.py
+++ b/solution.py
@@ -12,7 +12,8 @@
 LANES = 128
 ROWS = 32
 FINE = 16
-LAG = 5
+PARTS = 2
+LAG = 10
 ENTER = 256
 UNROLL = 4
 LEAVE = 256
@@ -157,7 +158,8 @@
     blocks = length // STEPS
     pairs, _, subs, fine, columns = all_ref.shape
     rows = subs * fine
-    count_of = pairs * subs
+    piece_columns = columns // PARTS
+    count_of = pairs * subs * PARTS
     span = lax.axis_index("span")
     me = lax.axis_index("tensor")
     core = lax.rem(me, 2)
@@ -390,14 +392,19 @@
     def multiply(pair):
         remote(active_ref.at[pair, 1 - core], mate_ref.at[pair], mate_send, mate_recv.at[pair], "tensor", partner).wait_recv()
         product = dot(active_ref[pair, core], weight_ref[0]) + dot(mate_ref[pair], weight_ref[1])
-        for sub in range(subs):
-            part_ref[pair * subs + sub] = product[sub * fine : (sub + 1) * fine]
+        cuts = [
+            product[sub * fine : (sub + 1) * fine, lanes]
+            for sub in range(subs)
+            for lanes in lanes_of(columns, piece_columns)
+        ]
+        for spot, cut in enumerate(cuts):
+            part_ref[pair * subs * PARTS + spot] = cut
 
         @pl.when(end)
         def _():
-            for sub in range(subs):
-                item = pair * subs + sub
-                hop_ref[near, item] = product[sub * fine : (sub + 1) * fine].astype(jnp.bfloat16)
+            for spot, cut in enumerate(cuts):
+                item = pair * subs * PARTS + spot
+                hop_ref[near, item] = cut.astype(jnp.bfloat16)
                 hop(near, item, inner).start()
 
     for pair in range(pairs):
@@ -433,10 +440,14 @@
             hop_ref[far, item] = running.astype(jnp.bfloat16)
             hop(far, item, outer).start()
 
-        shared = running + land_ref[near, item].astype(jnp.float32)
-        squares = jnp.mean(shared * shared, axis=1, keepdims=True)
-        all_ref[item // subs, core, item % subs] = (shared * lax.rsqrt(squares + SCALE_EPS) * gain_ref[...]).astype(jnp.bfloat16)
-        home(item).start()
+        return running + land_ref[near, item].astype(jnp.float32)
+
+    def settle(block, halves):
+        squares = sum(jnp.sum(half * half, axis=1, keepdims=True) for half in halves) / columns
+        scale = lax.rsqrt(squares + SCALE_EPS)
+        for half, lanes in zip(halves, lanes_of(columns, piece_columns)):
+            all_ref[block // subs, core, block % subs, :, lanes] = (half * scale * gain_ref[:, lanes]).astype(jnp.bfloat16)
+        home(block).start()
 
     def finish(pair):
         slot = all_ref.at[pair, core]
@@ -444,14 +455,19 @@
         gathered = all_ref[pair].reshape(2 * rows, columns)
         out_ref[2 * pair * rows : 2 * (pair + 1) * rows, :] = dot(gathered, mixer_ref[...]).astype(jnp.bfloat16)
 
+    held = []
     for item in range(count_of + LAG):
         if item < count_of:
             relay(item)
         item -= LAG
         if item >= 0:
-            close(item)
-            if item % subs == subs - 1 and item >= subs:
-                finish(item // subs - 1)
+            held.append(close(item))
+            if len(held) == PARTS:
+                block = item // PARTS
+                settle(block, held)
+                held = []
+                if block % subs == subs - 1 and block >= subs:
+                    finish(block // subs - 1)
     finish(pairs - 1)
 
     sent_later(count, *stats)
@@ -474,7 +490,7 @@
     chips = lax.axis_size("tensor") // 2
     columns = weight.shape[1]
     pairs = length // (2 * ROWS)
-    items = length // (2 * FINE)
+    items = PARTS * length // (2 * FINE)
     f32, bf16 = jnp.float32, jnp.bfloat16
     sems = pltpu.SemaphoreType.DMA
     hbm = pl.BlockSpec(memory_space=pltpu.HBM)
@@ -519,9 +535,9 @@
             pltpu.VMEM((length, channels), f32),
             pltpu.VMEM((pairs, 2, ROWS, channels), bf16),
             pltpu.VMEM((pairs, ROWS, channels), bf16),
-            pltpu.VMEM((items, FINE, columns), f32),
-            pltpu.VMEM((2, items, FINE, columns), bf16),
-            pltpu.VMEM((2, items, FINE, columns), bf16),
+            pltpu.VMEM((items, FINE, columns // PARTS), f32),
+            pltpu.VMEM((2, items, FINE, columns // PARTS), bf16),
+            pltpu.VMEM((2, items, FINE, columns // PARTS), bf16),
             pltpu.VMEM((pairs, 2, ROWS // FINE, FINE, columns), bf16),
             sems((4,)),
             sems(()),

time: 29.6 us -> 29.4 us (level)
  Pallas kernels: 28.8 us -> 28.5 us
where the time goes in v4:
time: 29.4 us; the launch traced here: 29.2 us
  Pallas kernels  28.5 us (97%)
  local copies, waits for them, and re-layouts  0.71 us (2%)
    pallas_call x1, Pallas kernels, layer(): pl.pallas_call(functools.partial(layer_kernel, count, chips), out_shape=p...  28.5 us
    unnamed x1, local copies, waits for them, and re-layouts  0.71 us

profile of v4, /device:TPU:5, one launch (start us, length us, event | category | flops | bytes accessed | tf_op | source)
XLA Modules:
  0.0 29.2 jit_solution(4596283750193092498)
XLA Ops:
  0.0 28.5 %layer.1 = bf16[256,512]{1,0:T(8,128)(2,1)S(1)} custom-call(bf16[256,512]{1,0:T(8,128)(2,1)} %tokens_hbm.1, f32[1,256]{1,0:T(1,128)} %bitcast.9, f32[1,512]{1,0:T(1,128)} %bitcast.6, f32[1,512]{1,0:T(1,128)} %bitcast.7, f32[16,512]{1,0:T(8,128)} %rate_hbm.1, f32[16,512]{1,0:T(8,128)} %angle_hbm.1, f32[16,512]{1,0:T(8,128)} %input_hbm.1, ...), custom_call_target="tpu_custom_call" | custom-call | tf_op jit(solution)/shard_map/layer/pallas_call | solution.py:512
  28.5 0.7 %copy.14 = bf16[256,512]{1,0:T(8,128)(2,1)} copy(bf16[256,512]{1,0:T(8,128)(2,1)S(1)} %layer.1) | data formatting | bytes 524288

commit v5 on v4

--- a/solution.py
+++ b/solution.py
@@ -13,9 +13,9 @@
 ROWS = 32
 FINE = 16
 PARTS = 2
-LAG = 10
+LAG = 12
 ENTER = 256
-UNROLL = 4
+UNROLL = 8
 LEAVE = 256
 NORM_EPS = 1e-05
 SCALE_EPS = 1e-06
@@ -228,7 +228,6 @@
     stats = (total_ref, totals_ref, total_send, total_recv)
     to_later(count, *stats)
     swap = remote(weight_hbm, weight_ref.at[1], weight_send, weight_recv, "tensor", partner)
-    swap.start()
 
     for load in loads[2:10]:
         load.wait()
@@ -285,6 +284,7 @@
     share = wide(1.0 / ((span * length + position + 1) * GROUP).astype(jnp.float32), channels)
 
     from_earlier(count, *stats)
+    swap.start()
     before_ref[...] = jnp.zeros((8, channels), jnp.float32)
     for other in range(count - 1):
 
@@ -449,11 +449,19 @@
             all_ref[block // subs, core, block % subs, :, lanes] = (half * scale * gain_ref[:, lanes]).astype(jnp.bfloat16)
         home(block).start()
 
-    def finish(pair):
+    def arrived(pair):
         slot = all_ref.at[pair, core]
         remote(slot, slot, home_send, home_recv.at[pair], "tensor", partner).wait_recv()
+
+    def finish(pair):
+        arrived(pair)
         gathered = all_ref[pair].reshape(2 * rows, columns)
         out_ref[2 * pair * rows : 2 * (pair + 1) * rows, :] = dot(gathered, mixer_ref[...]).astype(jnp.bfloat16)
+
+    def finish_side(pair, side):
+        gathered = all_ref[pair, side].reshape(rows, columns)
+        first = pl.multiple_of((2 * pair + side) * rows, rows)
+        out_ref[pl.ds(first, rows), :] = dot(gathered, mixer_ref[...]).astype(jnp.bfloat16)
 
     held = []
     for item in range(count_of + LAG):
@@ -468,7 +476,9 @@
                 held = []
                 if block % subs == subs - 1 and block >= subs:
                     finish(block // subs - 1)
-    finish(pairs - 1)
+    finish_side(pairs - 1, core)
+    arrived(pairs - 1)
+    finish_side(pairs - 1, 1 - core)
 
     sent_later(count, *stats)
     sent_later(count, *states)

time: 29.4 us -> 29.3 us (level)
  no operation moved by 1% of the time
where the time goes in v5:
time: 29.3 us; the launch traced here: 29.1 us
  Pallas kernels  28.4 us (97%)
  local copies, waits for them, and re-layouts  0.71 us (2%)
    pallas_call x1, Pallas kernels, layer(): pl.pallas_call(functools.partial(layer_kernel, count, chips), out_shape=p...  28.4 us
    unnamed x1, local copies, waits for them, and re-layouts  0.71 us

profile of v5, /device:TPU:5, one launch (start us, length us, event | category | flops | bytes accessed | tf_op | source)
XLA Modules:
  0.0 29.1 jit_solution(7518951235568139397)
XLA Ops:
  0.0 28.4 %layer.1 = bf16[256,512]{1,0:T(8,128)(2,1)S(1)} custom-call(bf16[256,512]{1,0:T(8,128)(2,1)} %tokens_hbm.1, f32[1,256]{1,0:T(1,128)} %bitcast.9, f32[1,512]{1,0:T(1,128)} %bitcast.6, f32[1,512]{1,0:T(1,128)} %bitcast.7, f32[16,512]{1,0:T(8,128)} %rate_hbm.1, f32[16,512]{1,0:T(8,128)} %angle_hbm.1, f32[16,512]{1,0:T(8,128)} %input_hbm.1, ...), custom_call_target="tpu_custom_call" | custom-call | tf_op jit(solution)/shard_map/layer/pallas_call | solution.py:522
  28.4 0.7 %copy.14 = bf16[256,512]{1,0:T(8,128)(2,1)} copy(bf16[256,512]{1,0:T(8,128)(2,1)S(1)} %layer.1) | data formatting | bytes 524288
